TPU v7x, 128 devices: a whole 4x4x4 slice. The times are simulated.
128 devices in a mesh: dp: 8 (over x, core), space: 16 (over y, z).
Axes of the slice: x: 4, y: 4, z: 4, core: 2. Of those that a mesh axis runs over, the one named last changes fastest.
Arguments:
- layer_input: bfloat16 [8, 64, 32, 1024], P('dp', None, 'space'), may hold values from -6 to 6
- hidden_pre: bfloat16 [8, 128, 32, 1024], P('dp', None, 'space'), may hold values from -6 to 6
- output_pre: bfloat16 [8, 256, 16, 256], P('dp', None, 'space'), may hold values from -6 to 6
- output_grad: bfloat16 [8, 256, 16, 256], P('dp', None, 'space'), may hold values from -48 to 48
- weight_a: bfloat16 [27, 64, 128], replicated, may hold values from -0.15625 to 0.15625
- weight_b: bfloat16 [27, 128, 256], replicated, may hold values from -0.109375 to 0.109375
Outputs:
- input_grad: bfloat16 [8, 64, 32, 1024], P('dp', None, 'space')
- weight_grad_a: float32 [27, 64, 128], replicated
- weight_grad_b: float32 [27, 128, 256], replicated
All inputs are finite; a program needn't handle non-finite values.
Results may differ from a plain program's by a relative error of at most 0.013.
Values may be sent and summed in bfloat16 or wider, within the bound.
A program may use at most 64 MiB of HBM per device.

v0:
```python
import math
import jax
import jax.numpy as jnp
from jax import lax
from jax.sharding import PartitionSpec as P

negative_slope = 0.3


def padded_2(cells, sides, width):
    for axis, dim in sides:
        count = lax.axis_size(axis)
        ends = count - 1
        head = lax.slice_in_dim(cells, 0, width, axis=dim)
        tail = lax.slice_in_dim(cells, cells.shape[dim] - width, cells.shape[dim], axis=dim)
        cells = jnp.concatenate(
            [
                lax.ppermute(tail, axis, [(i, (i + 1) % count) for i in range(ends)]),
                cells,
                lax.ppermute(head, axis, [((i + 1) % count, i) for i in range(ends)]),
            ],
            axis=dim,
        )
    return cells


def slopes(values):
    return jnp.where(values > 0, jnp.ones_like(values), negative_slope * jnp.ones_like(values))


def window(padded, tap_z, tap_y, tap_x, depth, side):
    planes = padded[:, tap_z : tap_z + depth, :]
    margin = side + 1
    wider = jnp.pad(planes, ((0, 0), (0, 0), (margin, margin)))
    offset = (tap_y - 1) * side + (tap_x - 1)
    piece = wider[:, :, margin + offset : margin + offset + side * side]
    column = jnp.arange(side * side, dtype=jnp.int32) % side + (tap_x - 1)
    inside = (column >= 0) & (column < side)
    piece = jnp.where(inside, piece, jnp.zeros_like(piece))
    return piece.reshape(padded.shape[0], depth * side * side)


def outer_product(left, right):
    return lax.dot_general(
        left, right, (((1,), (1,)), ((), ())), preferred_element_type=jnp.float32
    )


def per_device(layer_input, hidden_pre, output_pre, output_grad, weight_a, weight_b):
    side = math.isqrt(layer_input.shape[3])
    half = side // 2
    depth_a = layer_input.shape[2]
    depth_b = depth_a // 2
    source = layer_input[0]
    hidden = hidden_pre[0]
    outer = output_pre[0]
    upstream = output_grad[0]
    chan_in = source.shape[0]
    width_a = hidden.shape[0]
    width_b = outer.shape[0]
    grad_outer = (upstream.astype(jnp.float32) * slopes(outer.astype(jnp.float32))).astype(
        jnp.bfloat16
    )
    hidden_f = hidden.astype(jnp.float32)
    active = jnp.where(hidden_f > 0, hidden_f, negative_slope * hidden_f)
    pooled = (
        active.reshape(width_a, depth_b, 2, half, 2, half, 2)
        .mean(axis=(2, 4, 6))
        .astype(jnp.bfloat16)
    )
    pooled = pooled.reshape(width_a, depth_b, half * half)
    outer_pad = padded_2(grad_outer, (("space", 1),), 1)
    pooled_pad = padded_2(pooled, (("space", 1),), 1)
    grad_flat = grad_outer.reshape(width_b, depth_b * half * half)
    back_b = jnp.zeros((width_a, depth_b * half * half), jnp.float32)
    terms_b = []
    for tap in range(27):
        tap_z, tap_y, tap_x = (tap // 9, tap // 3 % 3, tap % 3)
        mirror = window(outer_pad, 2 - tap_z, 2 - tap_y, 2 - tap_x, depth_b, half)
        back_b = back_b + jnp.dot(weight_b[tap], mirror, preferred_element_type=jnp.float32)
        terms_b.append(
            outer_product(window(pooled_pad, tap_z, tap_y, tap_x, depth_b, half), grad_flat)
        )
    sums_b = jnp.stack(terms_b)
    coarse = back_b.reshape(width_a, depth_b, half, half)
    upward = jnp.repeat(jnp.repeat(jnp.repeat(coarse, 2, 1), 2, 2), 2, 3) * 0.125
    upward = upward.reshape(width_a, depth_a * side * side)
    grad_hidden = (upward * slopes(hidden_f.reshape(width_a, depth_a * side * side))).astype(
        jnp.bfloat16
    )
    grad_hidden = grad_hidden.reshape(width_a, depth_a, side * side)
    hidden_pad = padded_2(grad_hidden, (("space", 1),), 1)
    source_pad = padded_2(source, (("space", 1),), 1)
    hidden_flat = grad_hidden.reshape(width_a, depth_a * side * side)
    back_a = jnp.zeros((chan_in, depth_a * side * side), jnp.float32)
    terms_a = []
    for tap in range(27):
        tap_z, tap_y, tap_x = (tap // 9, tap // 3 % 3, tap % 3)
        mirror = window(hidden_pad, 2 - tap_z, 2 - tap_y, 2 - tap_x, depth_a, side)
        back_a = back_a + jnp.dot(weight_a[tap], mirror, preferred_element_type=jnp.float32)
        terms_a.append(
            outer_product(window(source_pad, tap_z, tap_y, tap_x, depth_a, side), hidden_flat)
        )
    sums_a = jnp.stack(terms_a)
    input_grad = back_a.astype(jnp.bfloat16).reshape(1, chan_in, depth_a, side * side)
    total_a, total_b = lax.psum((sums_a, sums_b), ("dp", "space"))
    samples = lax.axis_size("dp")
    planes_a = depth_a * lax.axis_size("space")
    scale_a = 1.0 / math.sqrt(samples * planes_a * side * side)
    scale_b = 1.0 / math.sqrt(samples * (planes_a // 2) * half * half)
    return (input_grad, total_a * scale_a, total_b * scale_b)


def solution(mesh):
    in_specs = (
        P("dp", None, "space", None),
        P("dp", None, "space", None),
        P("dp", None, "space", None),
        P("dp", None, "space", None),
        P(),
        P(),
    )
    out_specs = (P("dp", None, "space", None), P(), P())
    return jax.shard_map(
        per_device, mesh=mesh, in_specs=in_specs, out_specs=out_specs, check_vma=False
    )
```

profile of v0, /device:TPU:1, one launch (start us, length us, event | category | flops | bytes accessed | tf_op | source)
XLA Modules:
  0.0 248.0 jit_solution(2244934263055690898)
XLA Ops:
  7.2 1.1 multiply_convert_fusion.1
  8.3 4.4 %collective-permute-start.1 = (bf16[256,1,256]{2,0,1:T(8,128)(2,1)S(1)}, bf16[256,1,256]{2,0,1:T(8,128)(2,1)S(1)}, u32[]{:S(2)}, u32[]{:S(2)}) collective-permute-start(bf16[256,1,256]{2,0,1:T(8,128)(2,1)S(1)} %bitcast.918), channel_id=1, source_target_pairs={{0,1},{1,2},{2,3},{3,4},{4,5},{5,6},{6,7},{7,8},{8,9},{9,10},{10,1... | collective-permute-start | bytes 393224 | tf_op jit(solution)/shard_map/ppermute | solution.py:18
  12.7 1.3 collective-permute-start
  14.0 1.4 copy.37
  15.6 0.4 reduce_sum.18
  16.0 4.2 %collective-permute-start.6 = (bf16[128,1,256]{0,2,1:T(8,128)(2,1)S(1)}, bf16[128,1,256]{0,2,1:T(8,128)(2,1)S(1)}, u32[]{:S(2)}, u32[]{:S(2)}) collective-permute-start(bf16[128,1,256]{0,2,1:T(8,128)(2,1)S(1)} %bitcast.928), channel_id=1, source_target_pairs={{0,1},{1,2},{2,3},{3,4},{4,5},{5,6},{6,7},{7,8},{8,9},{9,10},{10,1... | collective-permute-start | bytes 196616 | tf_op jit(solution)/shard_map/ppermute | solution.py:18
  20.2 1.3 collective-permute-start.7
  21.5 1.2 fusion.578
  22.6 1.3 collective-permute-start.5
  24.2 1.3 broadcast_select_fusion.7
  26.0 4.6 %collective-permute-start.4 = (bf16[64,1,1024]{2,1,0:T(2,128)(2,1)}, bf16[64,1,1024]{2,1,0:T(2,128)(2,1)S(1)}, u32[]{:S(2)}, u32[]{:S(2)}) collective-permute-start(bf16[64,1,1024]{2,1,0:T(2,128)(2,1)} %get-tuple-element.96), channel_id=1, source_target_pairs={{0,1},{1,2},{2,3},{3,4},{4,5},{5,6},{6,7},{7,8},{8,9},{9,10},{10,1... | collective-permute-start | bytes 393224 | tf_op jit(solution)/shard_map/ppermute | solution.py:18
  38.4 0.3 fusion.96
  38.7 0.3 fusion.86
  39.0 0.3 convolution_add_fusion.30
  39.3 0.3 convolution_add_fusion.29
  39.6 0.3 convolution_add_fusion.28
  40.2 0.3 convolution_add_fusion.26
  40.5 0.3 convolution_add_fusion.25
  40.8 0.3 convolution_add_fusion.24
  41.1 0.3 convolution_add_fusion.23
  41.5 0.3 convolution_add_fusion.22
  41.8 0.3 convolution_add_fusion.21
  42.1 0.3 convolution_add_fusion.20
  42.6 0.3 convolution_add_fusion.18
  43.0 0.3 convolution_add_fusion.17
  43.3 0.3 fusion.48
  43.6 0.3 fusion.47
  43.9 0.3 convolution_bitcast_fusion.40
  44.2 0.3 fusion.46
  44.6 0.3 fusion.45
  44.9 0.3 fusion.44
  45.2 0.3 fusion.43
  45.7 0.3 fusion.41
  46.1 0.3 fusion.40
  46.4 0.3 fusion.51
  47.2 3.4 %collective-permute-start.3 = (bf16[128,1,1024]{0,2,1:T(8,128)(2,1)S(1)}, bf16[128,1,1024]{0,2,1:T(8,128)(2,1)S(1)}, u32[]{:S(2)}, u32[]{:S(2)}) collective-permute-start(bf16[128,1,1024]{0,2,1:T(8,128)(2,1)S(1)} %get-tuple-element.54), channel_id=1, source_target_pairs={{0,1},{1,2},{2,3},{3,4},{4,5},{5,6},{6,7},{7,8},{8,9},{9,10},{10,1... | collective-permute-start | bytes 786440 | tf_op jit(solution)/shard_map/ppermute | solution.py:18
  50.6 1.5 collective-permute-start.2
  52.1 4.2 %broadcast_select_fusion.14 = (bf16[64,2,1024]{2,1,0:T(2,128)(2,1)S(1)}, bf16[64,2,1024]{2,1,0:T(2,128)(2,1)S(1)}, bf16[64,2,1024]{2,1,0:T(2,128)(2,1)S(1)}, bf1...) fusion(pred[1024]{0:T(1024)(128)(4,1)S(1)} %fusion.521, ...), kind=kLoop, calls=%fused_computation.231 | loop fusion | flops 1966080 | bytes 2885632 | tf_op jit(solution)/shard_map/jit(_where)/select_n | solution.py:39
  56.3 2.9 %broadcast_select_fusion.10 = (bf16[64,2,1024]{2,1,0:T(2,128)(2,1)S(1)}, bf16[64,2,1024]{2,1,0:T(2,128)(2,1)S(1)}, bf16[64,2,1024]{2,1,0:T(2,128)(2,1)S(1)}, bf1...) fusion(pred[1024]{0:T(1024)(128)(4,1)S(1)} %get-tuple-element.1, ...), kind=kLoop, calls=%fused_computation.227 | loop fusion | flops 1048576 | bytes 2362368 | tf_op jit(solution)/shard_map/jit(_where)/select_n | solution.py:39
  60.0 2.9 %broadcast_select_fusion.4 = (bf16[64,2,1024]{2,1,0:T(2,128)(2,1)S(1)}, bf16[64,2,1024]{2,1,0:T(2,128)(2,1)S(1)}, bf16[64,2,1024]{2,1,0:T(2,128)(2,1)S(1)}, bf16...) fusion(pred[1024]{0:T(1024)(128)(4,1)S(1)} %get-tuple-element.1, ...), kind=kLoop, calls=%fused_computation.221 | loop fusion | flops 1048576 | bytes 2362368 | tf_op jit(solution)/shard_map/jit(_where)/select_n | solution.py:39
  63.4 1.2 broadcast_select_fusion
  70.7 0.9 copy-done.3
  71.7 2.5 %broadcast_select_fusion.1 = (bf16[128,2,1024]{0,2,1:T(8,128)(2,1)S(1)}, bf16[128,2,1024]{0,2,1:T(8,128)(2,1)S(1)}, bf16[128,2,1024]{0,2,1:T(8,128)(2,1)S(1)}, b...) fusion(pred[1024]{0:T(1024)(128)(4,1)S(1)} %fusion.521, ...), kind=kLoop, calls=%fused_computation.218 | loop fusion | flops 4718592 | bytes 7343104 | tf_op jit(solution)/shard_map/jit(_where)/select_n | solution.py:39
  74.2 3.7 %slice_select_fusion.16 = (bf16[128,2,1024]{0,2,1:T(8,128)(2,1)S(1)}, bf16[128,2,1024]{0,2,1:T(8,128)(2,1)S(1)}, bf16[128,2,1024]{0,2,1:T(8,128)(2,1)S(1)}, bf16...) fusion(pred[1024]{0:T(1024)(128)(4,1)S(1)} %get-tuple-element.1, ...), kind=kLoop, calls=%fused_computation.210 | loop fusion | flops 4194304 | bytes 9440256 | tf_op jit(solution)/shard_map/jit(_where)/select_n | solution.py:39
  78.2 0.3 convolution_add_fusion.15
  78.6 0.3 convolution_add_fusion.14
  78.9 0.3 convolution_add_fusion.13
  79.2 0.3 convolution_add_fusion.12
  79.5 0.3 convolution_add_fusion.11
  80.1 0.3 convolution_add_fusion.9
  80.4 0.3 convolution_add_fusion.8
  81.0 0.3 convolution_add_fusion.6
  81.3 0.3 convolution_add_fusion.5
  82.2 0.3 convolution_add_fusion.2
  82.5 0.3 convolution_add_fusion.1
  82.8 0.3 fusion.10
  84.3 0.3 fusion.5
  84.6 0.3 fusion.4
  85.2 0.3 fusion.2
  85.8 0.3 fusion.11
  86.1 0.9 reshape.926
  87.0 147.7 %all-reduce.15.cloned.1.call-done = (f32[27,64,128]{2,1,0:T(8,128)}, f32[27,128,256]{2,1,0:T(8,128)}) async-done(((f32[27,64,128]{2,1,0:T(8,128)}, f32[27,128,256]{2,1,0:T(8,128)}), (f32[27,64,128]{2,1,0:T(8,128)}, f32[27,128,256]{2,1,0:T(8,128)})) %all-reduce.15.cloned.1.call-update) | async-done | bytes 4423696 | tf_op jit(solution)/shard_map/psum | solution.py:106
  234.7 2.2 broadcast_multiply_fusion.1
  236.9 4.3 %broadcast_multiply_fusion = f32[27,128,256]{2,1,0:T(8,128)} fusion(f32[27,128,256]{2,1,0:T(8,128)} %get-tuple-element.4), kind=kLoop, calls=%fused_computation.38 | loop fusion | flops 884736 | bytes 7077888 | tf_op jit(solution)/shard_map/mul | solution.py:111
  (128 shorter events, 20.3 us)
Async XLA Ops:
  7.2 14.3 %copy-start = (bf16[1,64,2,1024]{3,2,1,0:T(2,128)(2,1)S(1)}, bf16[1,64,2,1024]{3,2,1,0:T(2,128)(2,1)}, u32[]{:S(2)}) copy-start(bf16[1,64,2,1024]{3,2,1,0:T(2,128)(2,1)} %param.6) | copy-start | bytes 786436
  7.2 227.5 %all-reduce.15.cloned.1.call-start = ((), (), s32[]{:S(2)}) async-start(), calls=%async_computation | async-start | bytes 8847360 | tf_op jit(solution)/shard_map/psum | solution.py:106
  8.3 35.6 %collective-permute-start.1 = (bf16[256,1,256]{2,0,1:T(8,128)(2,1)S(1)}, bf16[256,1,256]{2,0,1:T(8,128)(2,1)S(1)}, u32[]{:S(2)}, u32[]{:S(2)}) collective-permute-start(bf16[256,1,256]{2,0,1:T(8,128)(2,1)S(1)} %bitcast.918), channel_id=1, source_target_pairs={{0,1},{1,2},{2,3},{3,4},{4,5},{5,6},{6,7},{7,8},{8,9},{9,10},{10,1... | collective-permute-start | bytes 393224 | tf_op jit(solution)/shard_map/ppermute | solution.py:18
  12.7 25.7 %collective-permute-start = (bf16[256,1,256]{2,0,1:T(8,128)(2,1)S(1)}, bf16[256,1,256]{2,0,1:T(8,128)(2,1)S(1)}, u32[]{:S(2)}, u32[]{:S(2)}) collective-permute-start(bf16[256,1,256]{2,0,1:T(8,128)(2,1)S(1)} %bitcast.919), channel_id=1, source_target_pairs={{1,0},{2,1},{3,2},{4,3},{5,4},{6,5},{7,6},{8,7},{9,8},{10,9},{11,1... | collective-permute-start | bytes 393224 | tf_op jit(solution)/shard_map/ppermute | solution.py:20
  16.0 10.0 %collective-permute-start.6 = (bf16[128,1,256]{0,2,1:T(8,128)(2,1)S(1)}, bf16[128,1,256]{0,2,1:T(8,128)(2,1)S(1)}, u32[]{:S(2)}, u32[]{:S(2)}) collective-permute-start(bf16[128,1,256]{0,2,1:T(8,128)(2,1)S(1)} %bitcast.928), channel_id=1, source_target_pairs={{0,1},{1,2},{2,3},{3,4},{4,5},{5,6},{6,7},{7,8},{8,9},{9,10},{10,1... | collective-permute-start | bytes 196616 | tf_op jit(solution)/shard_map/ppermute | solution.py:18
  20.2 15.6 %collective-permute-start.7 = (bf16[128,1,256]{0,2,1:T(8,128)(2,1)S(1)}, bf16[128,1,256]{0,2,1:T(8,128)(2,1)S(1)}, u32[]{:S(2)}, u32[]{:S(2)}) collective-permute-start(bf16[128,1,256]{0,2,1:T(8,128)(2,1)S(1)} %bitcast.929), channel_id=1, source_target_pairs={{1,0},{2,1},{3,2},{4,3},{5,4},{6,5},{7,6},{8,7},{9,8},{10,9},{11,1... | collective-permute-start | bytes 196616 | tf_op jit(solution)/shard_map/ppermute | solution.py:20
  22.6 29.5 %collective-permute-start.5 = (bf16[64,1,1024]{2,1,0:T(2,128)(2,1)}, bf16[64,1,1024]{2,1,0:T(2,128)(2,1)}, u32[]{:S(2)}, u32[]{:S(2)}) collective-permute-start(bf16[64,1,1024]{2,1,0:T(2,128)(2,1)} %get-tuple-element.95), channel_id=1, source_target_pairs={{1,0},{2,1},{3,2},{4,3},{5,4},{6,5},{7,6},{8,7},{9,8},{10,9},{11,1... | collective-permute-start | bytes 393224 | tf_op jit(solution)/shard_map/ppermute | solution.py:20
  26.0 26.1 %collective-permute-start.4 = (bf16[64,1,1024]{2,1,0:T(2,128)(2,1)}, bf16[64,1,1024]{2,1,0:T(2,128)(2,1)S(1)}, u32[]{:S(2)}, u32[]{:S(2)}) collective-permute-start(bf16[64,1,1024]{2,1,0:T(2,128)(2,1)} %get-tuple-element.96), channel_id=1, source_target_pairs={{0,1},{1,2},{2,3},{3,4},{4,5},{5,6},{6,7},{7,8},{8,9},{9,10},{10,1... | collective-permute-start | bytes 393224 | tf_op jit(solution)/shard_map/ppermute | solution.py:18
  32.0 6.3 %copy-start.2 = (bf16[27,128,256]{2,1,0:T(8,128)(2,1)S(1)}, bf16[27,128,256]{2,1,0:T(8,128)(2,1)}, u32[]{:S(2)}) copy-start(bf16[27,128,256]{2,1,0:T(8,128)(2,1)} %param.11) | copy-start | bytes 5308420
  38.3 4.9 %copy-start.1 = (f32[27,128,256]{2,1,0:T(8,128)}, f32[27,128,256]{2,1,0:T(8,128)S(1)}, u32[]{:S(2)}) copy-start(f32[27,128,256]{2,1,0:T(8,128)S(1)} %fusion.12) | copy-start | bytes 10616836
  47.2 24.4 %collective-permute-start.3 = (bf16[128,1,1024]{0,2,1:T(8,128)(2,1)S(1)}, bf16[128,1,1024]{0,2,1:T(8,128)(2,1)S(1)}, u32[]{:S(2)}, u32[]{:S(2)}) collective-permute-start(bf16[128,1,1024]{0,2,1:T(8,128)(2,1)S(1)} %get-tuple-element.54), channel_id=1, source_target_pairs={{0,1},{1,2},{2,3},{3,4},{4,5},{5,6},{6,7},{7,8},{8,9},{9,10},{10,1... | collective-permute-start | bytes 786440 | tf_op jit(solution)/shard_map/ppermute | solution.py:18
  50.6 21.1 %collective-permute-start.2 = (bf16[128,1,1024]{0,2,1:T(8,128)(2,1)S(1)}, bf16[128,1,1024]{0,2,1:T(8,128)(2,1)S(1)}, u32[]{:S(2)}, u32[]{:S(2)}) collective-permute-start(bf16[128,1,1024]{0,2,1:T(8,128)(2,1)S(1)} %get-tuple-element.55), channel_id=1, source_target_pairs={{1,0},{2,1},{3,2},{4,3},{5,4},{6,5},{7,6},{8,7},{9,8},{10,9},{11,1... | collective-permute-start | bytes 786440 | tf_op jit(solution)/shard_map/ppermute | solution.py:20
  70.7 0.9 copy-start.3
  74.2 3.7 %copy-start.4 = (bf16[27,64,128]{2,1,0:T(8,128)(2,1)S(1)}, bf16[27,64,128]{2,1,0:T(8,128)(2,1)}, u32[]{:S(2)}) copy-start(bf16[27,64,128]{2,1,0:T(8,128)(2,1)} %param.10) | copy-start | bytes 1327108
Sparse Core Ops, SparseCore 0:
  71.8 162.8 all-reduce.14
where the time goes:
time: 248 us
  waiting for transfers between devices  148 us (60%)
  matrix products  29.7 us (12%)
  other arithmetic  27.2 us (11%)
  starting transfers between devices  21.9 us (9%)
  between operations  15.2 us (6%)
  local copies, waits for them, and re-layouts  6.3 us (3%)
    psum x1, waiting for transfers between devices, per_device(): total_a, total_b = lax.psum((sums_a, sums_b), ('dp', 'space'))  148 us
    select_n x8, other arithmetic, window(): piece = jnp.where(inside, piece, jnp.zeros_like(piece))  18.8 us
    ppermute x4, starting transfers between devices, padded_2(): lax.ppermute(tail, axis, [(i, (i + 1) % count) for i in range(ends)])  16.5 us
    dot_general x54, matrix products, outer_product(): lax.dot_general(left, right, (((1,), (1,)), ((), ())), preferred_element_...  13.6 us
    dot_general x27, matrix products, per_device(): jnp.dot(weight_b[tap], mirror, preferred_element_type=jnp.float32)  8.12 us
    dot_general x27, matrix products, per_device(): jnp.dot(weight_a[tap], mirror, preferred_element_type=jnp.float32)  8 us
    mul x2, other arithmetic, per_device(): return (input_grad, total_a * scale_a, total_b * scale_b)  6.44 us
    ppermute x4, starting transfers between devices, padded_2(): lax.ppermute(head, axis, [((i + 1) % count, i) for i in range(ends)])  5.34 us
  transfers between devices with their start and end apart: 9, of which 1 were waited for; matrix products, arithmetic and copies ran while one was open for 22% of the time, Pallas kernels for 0%

commit v1 on v0

--- a/solution.py
+++ b/solution.py
@@ -3,8 +3,14 @@
 import jax.numpy as jnp
 from jax import lax
 from jax.sharding import PartitionSpec as P
+from jax.lax import psum
 
 negative_slope = 0.3
+
+
+def _start_strings(buf, axis_name, chip_axis):
+    u1 = psum(psum(buf, axis_name), chip_axis)
+    return u1
 
 
 def padded_2(cells, sides, width):
@@ -103,7 +109,7 @@
         )
     sums_a = jnp.stack(terms_a)
     input_grad = back_a.astype(jnp.bfloat16).reshape(1, chan_in, depth_a, side * side)
-    total_a, total_b = lax.psum((sums_a, sums_b), ("dp", "space"))
+    total_a, total_b = _start_strings((sums_a, sums_b), "dp", "space")
     samples = lax.axis_size("dp")
     planes_a = depth_a * lax.axis_size("space")
     scale_a = 1.0 / math.sqrt(samples * planes_a * side * side)

time: 248 us -> 277 us (1.12)
  waiting for transfers between devices: 148 us -> 161 us
  matrix products: 29.7 us -> 41 us
  other arithmetic: 27.2 us -> 30 us
    psum x1 -> x2, waiting for transfers between devices: 148 us -> 161 us  [_start_strings(): u1 = psum(psum(buf, axis_name), chip_axis)]
    dot_general x27, matrix products: 8 us -> 19.3 us  [per_device(): jnp.dot(weight_a[tap], mirror, preferred_element_type=jnp.float32)]
    select_n x8, other arithmetic: 18.8 us -> 21.6 us  [window(): piece = jnp.where(inside, piece, jnp.zeros_like(piece))]
  transfers between devices with their start and end apart: 9 -> 10, of which waited for: 1 -> 2; matrix products, arithmetic and copies ran while one was open for 22% -> 25% of each run, Pallas kernels for 0% -> 0%
where the time goes in v1:
time: 277 us; the launch traced here: 276 us
  waiting for transfers between devices  161 us (58%)
  matrix products  41 us (15%)
  other arithmetic  30 us (11%)
  starting transfers between devices  22.2 us (8%)
  between operations  15.2 us (5%)
  local copies, waits for them, and re-layouts  6.25 us (2%)
    psum x2, waiting for transfers between devices, _start_strings(): u1 = psum(psum(buf, axis_name), chip_axis)  161 us
    select_n x8, other arithmetic, window(): piece = jnp.where(inside, piece, jnp.zeros_like(piece))  21.6 us
    dot_general x27, matrix products, per_device(): jnp.dot(weight_a[tap], mirror, preferred_element_type=jnp.float32)  19.3 us
    ppermute x4, starting transfers between devices, padded_2(): lax.ppermute(tail, axis, [(i, (i + 1) % count) for i in range(ends)])  16.5 us
    dot_general x54, matrix products, outer_product(): lax.dot_general(left, right, (((1,), (1,)), ((), ())), preferred_element_...  13.6 us
    dot_general x27, matrix products, per_device(): jnp.dot(weight_b[tap], mirror, preferred_element_type=jnp.float32)  8.12 us
    mul x2, other arithmetic, per_device(): return (input_grad, total_a * scale_a, total_b * scale_b)  6.44 us
  transfers between devices with their start and end apart: 10, of which 2 were waited for; matrix products, arithmetic and copies ran while one was open for 25% of the time, Pallas kernels for 0%

profile of v1, /device:TPU:1, one launch (start us, length us, event | category | flops | bytes accessed | tf_op | source)
XLA Modules:
  0.0 275.7 jit_solution(12487502570608366027)
XLA Ops:
  7.2 1.1 multiply_convert_fusion.1
  8.3 4.4 %collective-permute-start.1 = (bf16[256,1,256]{2,0,1:T(8,128)(2,1)S(1)}, bf16[256,1,256]{2,0,1:T(8,128)(2,1)S(1)}, u32[]{:S(2)}, u32[]{:S(2)}) collective-permute-start(bf16[256,1,256]{2,0,1:T(8,128)(2,1)S(1)} %bitcast.918), channel_id=1, source_target_pairs={{0,1},{1,2},{2,3},{3,4},{4,5},{5,6},{6,7},{7,8},{8,9},{9,10},{10,1... | collective-permute-start | bytes 393224 | tf_op jit(solution)/shard_map/ppermute | solution.py:24
  12.7 1.3 collective-permute-start
  14.0 1.4 copy.37
  15.6 0.4 reduce_sum.18
  16.0 4.2 %collective-permute-start.6 = (bf16[128,1,256]{0,2,1:T(8,128)(2,1)S(1)}, bf16[128,1,256]{0,2,1:T(8,128)(2,1)S(1)}, u32[]{:S(2)}, u32[]{:S(2)}) collective-permute-start(bf16[128,1,256]{0,2,1:T(8,128)(2,1)S(1)} %bitcast.928), channel_id=1, source_target_pairs={{0,1},{1,2},{2,3},{3,4},{4,5},{5,6},{6,7},{7,8},{8,9},{9,10},{10,1... | collective-permute-start | bytes 196616 | tf_op jit(solution)/shard_map/ppermute | solution.py:24
  20.2 1.3 collective-permute-start.7
  21.5 1.1 fusion.578
  22.5 1.3 collective-permute-start.5
  24.1 1.3 broadcast_select_fusion.7
  25.9 4.6 %collective-permute-start.4 = (bf16[64,1,1024]{2,1,0:T(2,128)(2,1)S(1)}, bf16[64,1,1024]{2,1,0:T(2,128)(2,1)S(1)}, u32[]{:S(2)}, u32[]{:S(2)}) collective-permute-start(bf16[64,1,1024]{2,1,0:T(2,128)(2,1)S(1)} %get-tuple-element.98), channel_id=1, source_target_pairs={{0,1},{1,2},{2,3},{3,4},{4,5},{5,6},{6,7},{7,8},{8,9},{9,10},{10,1... | collective-permute-start | bytes 393224 | tf_op jit(solution)/shard_map/ppermute | solution.py:24
  38.6 0.3 fusion.86
  38.9 0.3 convolution_add_fusion.30
  39.2 0.3 convolution_add_fusion.29
  39.5 0.3 convolution_add_fusion.28
  40.1 0.3 convolution_add_fusion.26
  40.4 0.3 convolution_add_fusion.25
  40.7 0.3 convolution_add_fusion.24
  41.0 0.3 convolution_add_fusion.23
  41.4 0.3 convolution_add_fusion.22
  41.7 0.3 convolution_add_fusion.21
  42.0 0.3 convolution_add_fusion.20
  42.5 0.3 convolution_add_fusion.18
  42.9 0.3 convolution_add_fusion.17
  43.2 0.3 fusion.48
  43.5 0.3 fusion.47
  44.1 0.3 fusion.46
  44.5 0.3 fusion.45
  44.8 0.3 fusion.44
  45.1 0.3 fusion.43
  45.6 0.3 fusion.41
  46.0 0.3 fusion.40
  46.3 0.3 fusion.51
  47.1 3.4 %collective-permute-start.3 = (bf16[128,1,1024]{0,2,1:T(8,128)(2,1)S(1)}, bf16[128,1,1024]{0,2,1:T(8,128)(2,1)S(1)}, u32[]{:S(2)}, u32[]{:S(2)}) collective-permute-start(bf16[128,1,1024]{0,2,1:T(8,128)(2,1)S(1)} %get-tuple-element.56), channel_id=1, source_target_pairs={{0,1},{1,2},{2,3},{3,4},{4,5},{5,6},{6,7},{7,8},{8,9},{9,10},{10,1... | collective-permute-start | bytes 786440 | tf_op jit(solution)/shard_map/ppermute | solution.py:24
  50.5 1.5 collective-permute-start.2
  52.0 4.2 %broadcast_select_fusion.14 = (bf16[64,2,1024]{2,1,0:T(2,128)(2,1)S(1)}, bf16[64,2,1024]{2,1,0:T(2,128)(2,1)S(1)}, bf16[64,2,1024]{2,1,0:T(2,128)(2,1)S(1)}, bf1...) fusion(pred[1024]{0:T(1024)(128)(4,1)S(1)} %fusion.521, ...), kind=kLoop, calls=%fused_computation.231 | loop fusion | flops 1966080 | bytes 2885632 | tf_op jit(solution)/shard_map/jit(_where)/select_n | solution.py:45
  56.2 2.9 %broadcast_select_fusion.10 = (bf16[64,2,1024]{2,1,0:T(2,128)(2,1)S(1)}, bf16[64,2,1024]{2,1,0:T(2,128)(2,1)S(1)}, bf16[64,2,1024]{2,1,0:T(2,128)(2,1)S(1)}, bf1...) fusion(pred[1024]{0:T(1024)(128)(4,1)S(1)} %get-tuple-element.1, ...), kind=kLoop, calls=%fused_computation.227 | loop fusion | flops 1048576 | bytes 2362368 | tf_op jit(solution)/shard_map/jit(_where)/select_n | solution.py:45
  59.9 2.9 %broadcast_select_fusion.4 = (bf16[64,2,1024]{2,1,0:T(2,128)(2,1)S(1)}, bf16[64,2,1024]{2,1,0:T(2,128)(2,1)S(1)}, bf16[64,2,1024]{2,1,0:T(2,128)(2,1)S(1)}, bf16...) fusion(pred[1024]{0:T(1024)(128)(4,1)S(1)} %get-tuple-element.1, ...), kind=kLoop, calls=%fused_computation.221 | loop fusion | flops 1048576 | bytes 2362368 | tf_op jit(solution)/shard_map/jit(_where)/select_n | solution.py:45
  63.3 1.2 broadcast_select_fusion
  70.6 0.9 copy-done.12
  71.9 4.7 %broadcast_select_fusion.1 = (bf16[128,2,1024]{0,2,1:T(8,128)(2,1)S(1)}, bf16[128,2,1024]{0,2,1:T(8,128)(2,1)S(1)}, bf16[128,2,1024]{0,2,1:T(8,128)(2,1)S(1)}, b...) fusion(pred[1024]{0:T(1024)(128)(4,1)S(1)} %fusion.521, ...), kind=kLoop, calls=%fused_computation.218 | loop fusion | flops 4718592 | bytes 7343104 | tf_op jit(solution)/shard_map/jit(_where)/select_n | solution.py:45
  76.5 4.4 %slice_select_fusion.16 = (bf16[128,2,1024]{0,2,1:T(8,128)(2,1)S(1)}, bf16[128,2,1024]{0,2,1:T(8,128)(2,1)S(1)}, bf16[128,2,1024]{0,2,1:T(8,128)(2,1)S(1)}, bf16...) fusion(pred[1024]{0:T(1024)(128)(4,1)S(1)} %get-tuple-element.1, ...), kind=kLoop, calls=%fused_computation.210 | loop fusion | flops 4194304 | bytes 9440256 | tf_op jit(solution)/shard_map/jit(_where)/select_n | solution.py:45
  80.9 1.0 fusion.477
  81.9 1.0 convolution_add_fusion.15
  82.9 1.0 convolution_add_fusion.14
  83.9 1.0 convolution_add_fusion.13
  85.0 1.0 convolution_add_fusion.12
  86.0 1.0 convolution_add_fusion.11
  87.0 1.0 convolution_add_fusion.10
  88.1 1.0 convolution_add_fusion.9
  89.1 1.0 convolution_add_fusion.8
  90.1 1.8 convolution_add_fusion.7
  91.9 59.1 %all-reduce.19.cloned.1.call-done = (f32[27,64,128]{2,1,0:T(8,128)}, f32[27,128,256]{2,1,0:T(8,128)}) async-done(((f32[27,64,128]{2,1,0:T(8,128)}, f32[27,128,256]{2,1,0:T(8,128)}), (f32[27,64,128]{2,1,0:T(8,128)}, f32[27,128,256]{2,1,0:T(8,128)})) %all-reduce.19.cloned.1.call-update) | async-done | bytes 4423696 | tf_op jit(solution)/shard_map/psum | solution.py:12
  151.1 1.6 convolution_add_fusion.6
  152.8 1.4 convolution_add_fusion.5
  154.2 1.1 convolution_add_fusion.4
  155.6 0.3 convolution_add_fusion.2
  155.9 0.3 convolution_add_fusion.1
  157.8 0.3 fusion.5
  158.1 0.3 fusion.4
  159.7 0.9 reshape.926
  160.5 101.9 %all-reduce.17.cloned.1.call-done = (f32[27,64,128]{2,1,0:T(8,128)}, f32[27,128,256]{2,1,0:T(8,128)}) async-done(((f32[27,64,128]{2,1,0:T(8,128)}, f32[27,128,256]{2,1,0:T(8,128)}), (f32[27,64,128]{2,1,0:T(8,128)}, f32[27,128,256]{2,1,0:T(8,128)})) %all-reduce.17.cloned.1.call-update) | async-done | bytes 4423696 | tf_op jit(solution)/shard_map/psum | solution.py:12
  262.4 2.2 broadcast_multiply_fusion.1
  264.6 4.3 %broadcast_multiply_fusion = f32[27,128,256]{2,1,0:T(8,128)} fusion(f32[27,128,256]{2,1,0:T(8,128)} %get-tuple-element.4), kind=kLoop, calls=%fused_computation.38 | loop fusion | flops 884736 | bytes 7077888 | tf_op jit(solution)/shard_map/mul | solution.py:117
  (149 shorter events, 20.9 us)
Async XLA Ops:
  7.2 14.3 %copy-start = (bf16[1,64,2,1024]{3,2,1,0:T(2,128)(2,1)S(1)}, bf16[1,64,2,1024]{3,2,1,0:T(2,128)(2,1)}, u32[]{:S(2)}) copy-start(bf16[1,64,2,1024]{3,2,1,0:T(2,128)(2,1)} %param.6) | copy-start | bytes 786436
  7.2 143.9 %all-reduce.19.cloned.1.call-start = ((), (), s32[]{:S(2)}) async-start(), calls=%async_computation.1 | async-start | bytes 8847360 | tf_op jit(solution)/shard_map/psum | solution.py:12
  8.3 35.5 %collective-permute-start.1 = (bf16[256,1,256]{2,0,1:T(8,128)(2,1)S(1)}, bf16[256,1,256]{2,0,1:T(8,128)(2,1)S(1)}, u32[]{:S(2)}, u32[]{:S(2)}) collective-permute-start(bf16[256,1,256]{2,0,1:T(8,128)(2,1)S(1)} %bitcast.918), channel_id=1, source_target_pairs={{0,1},{1,2},{2,3},{3,4},{4,5},{5,6},{6,7},{7,8},{8,9},{9,10},{10,1... | collective-permute-start | bytes 393224 | tf_op jit(solution)/shard_map/ppermute | solution.py:24
  12.7 25.6 %collective-permute-start = (bf16[256,1,256]{2,0,1:T(8,128)(2,1)S(1)}, bf16[256,1,256]{2,0,1:T(8,128)(2,1)S(1)}, u32[]{:S(2)}, u32[]{:S(2)}) collective-permute-start(bf16[256,1,256]{2,0,1:T(8,128)(2,1)S(1)} %bitcast.919), channel_id=1, source_target_pairs={{1,0},{2,1},{3,2},{4,3},{5,4},{6,5},{7,6},{8,7},{9,8},{10,9},{11,1... | collective-permute-start | bytes 393224 | tf_op jit(solution)/shard_map/ppermute | solution.py:26
  16.0 9.9 %collective-permute-start.6 = (bf16[128,1,256]{0,2,1:T(8,128)(2,1)S(1)}, bf16[128,1,256]{0,2,1:T(8,128)(2,1)S(1)}, u32[]{:S(2)}, u32[]{:S(2)}) collective-permute-start(bf16[128,1,256]{0,2,1:T(8,128)(2,1)S(1)} %bitcast.928), channel_id=1, source_target_pairs={{0,1},{1,2},{2,3},{3,4},{4,5},{5,6},{6,7},{7,8},{8,9},{9,10},{10,1... | collective-permute-start | bytes 196616 | tf_op jit(solution)/shard_map/ppermute | solution.py:24
  20.2 15.5 %collective-permute-start.7 = (bf16[128,1,256]{0,2,1:T(8,128)(2,1)S(1)}, bf16[128,1,256]{0,2,1:T(8,128)(2,1)S(1)}, u32[]{:S(2)}, u32[]{:S(2)}) collective-permute-start(bf16[128,1,256]{0,2,1:T(8,128)(2,1)S(1)} %bitcast.929), channel_id=1, source_target_pairs={{1,0},{2,1},{3,2},{4,3},{5,4},{6,5},{7,6},{8,7},{9,8},{10,9},{11,1... | collective-permute-start | bytes 196616 | tf_op jit(solution)/shard_map/ppermute | solution.py:26
  22.5 29.5 %collective-permute-start.5 = (bf16[64,1,1024]{2,1,0:T(2,128)(2,1)}, bf16[64,1,1024]{2,1,0:T(2,128)(2,1)}, u32[]{:S(2)}, u32[]{:S(2)}) collective-permute-start(bf16[64,1,1024]{2,1,0:T(2,128)(2,1)} %get-tuple-element.97), channel_id=1, source_target_pairs={{1,0},{2,1},{3,2},{4,3},{5,4},{6,5},{7,6},{8,7},{9,8},{10,9},{11,1... | collective-permute-start | bytes 393224 | tf_op jit(solution)/shard_map/ppermute | solution.py:26
  25.9 26.1 %collective-permute-start.4 = (bf16[64,1,1024]{2,1,0:T(2,128)(2,1)S(1)}, bf16[64,1,1024]{2,1,0:T(2,128)(2,1)S(1)}, u32[]{:S(2)}, u32[]{:S(2)}) collective-permute-start(bf16[64,1,1024]{2,1,0:T(2,128)(2,1)S(1)} %get-tuple-element.98), channel_id=1, source_target_pairs={{0,1},{1,2},{2,3},{3,4},{4,5},{5,6},{6,7},{7,8},{8,9},{9,10},{10,1... | collective-permute-start | bytes 393224 | tf_op jit(solution)/shard_map/ppermute | solution.py:24
  31.9 6.3 %copy-start.11 = (bf16[27,128,256]{2,1,0:T(8,128)(2,1)S(1)}, bf16[27,128,256]{2,1,0:T(8,128)(2,1)}, u32[]{:S(2)}) copy-start(bf16[27,128,256]{2,1,0:T(8,128)(2,1)} %param.11) | copy-start | bytes 5308420
  38.3 4.9 %copy-start.1 = (f32[27,128,256]{2,1,0:T(8,128)}, f32[27,128,256]{2,1,0:T(8,128)S(1)}, u32[]{:S(2)}) copy-start(f32[27,128,256]{2,1,0:T(8,128)S(1)} %fusion.12) | copy-start | bytes 10616836
  47.1 24.7 %collective-permute-start.3 = (bf16[128,1,1024]{0,2,1:T(8,128)(2,1)S(1)}, bf16[128,1,1024]{0,2,1:T(8,128)(2,1)S(1)}, u32[]{:S(2)}, u32[]{:S(2)}) collective-permute-start(bf16[128,1,1024]{0,2,1:T(8,128)(2,1)S(1)} %get-tuple-element.56), channel_id=1, source_target_pairs={{0,1},{1,2},{2,3},{3,4},{4,5},{5,6},{6,7},{7,8},{8,9},{9,10},{10,1... | collective-permute-start | bytes 786440 | tf_op jit(solution)/shard_map/ppermute | solution.py:24
  50.5 21.3 %collective-permute-start.2 = (bf16[128,1,1024]{0,2,1:T(8,128)(2,1)S(1)}, bf16[128,1,1024]{0,2,1:T(8,128)(2,1)}, u32[]{:S(2)}, u32[]{:S(2)}) collective-permute-start(bf16[128,1,1024]{0,2,1:T(8,128)(2,1)S(1)} %get-tuple-element.57), channel_id=1, source_target_pairs={{1,0},{2,1},{3,2},{4,3},{5,4},{6,5},{7,6},{8,7},{9,8},{10,9},{11,1... | collective-permute-start | bytes 786440 | tf_op jit(solution)/shard_map/ppermute | solution.py:26
  70.6 0.9 copy-start.12
  71.6 190.9 %all-reduce.17.cloned.1.call-start = ((), (), s32[]{:S(2)}) async-start(), calls=%async_computation | async-start | bytes 8847360 | tf_op jit(solution)/shard_map/psum | solution.py:12
  151.1 3.1 %copy-start.9 = (bf16[128,2,1024]{0,2,1:T(8,128)(2,1)S(1)}, bf16[128,2,1024]{0,2,1:T(8,128)(2,1)}, u32[]{:S(2)}) copy-start(bf16[128,2,1024]{0,2,1:T(8,128)(2,1)} %get-tuple-element.50) | copy-start | bytes 1572868
  151.1 4.2 %copy-start.13 = (bf16[27,64,128]{2,1,0:T(8,128)(2,1)S(1)}, bf16[27,64,128]{2,1,0:T(8,128)(2,1)}, u32[]{:S(2)}) copy-start(bf16[27,64,128]{2,1,0:T(8,128)(2,1)} %param.10) | copy-start | bytes 1327108
  151.1 4.5 %copy-start.5 = (bf16[128,2,1024]{0,2,1:T(8,128)(2,1)S(1)}, bf16[128,2,1024]{0,2,1:T(8,128)(2,1)}, u32[]{:S(2)}) copy-start(bf16[128,2,1024]{0,2,1:T(8,128)(2,1)} %get-tuple-element.53) | copy-start | bytes 1572868
  152.8 3.2 %copy-start.3 = (bf16[128,2,1024]{0,2,1:T(8,128)(2,1)S(1)}, bf16[128,2,1024]{0,2,1:T(8,128)(2,1)}, u32[]{:S(2)}) copy-start(bf16[128,2,1024]{0,2,1:T(8,128)(2,1)} %get-tuple-element.52) | copy-start | bytes 1572868
  154.2 2.1 copy-start.2
  155.6 1.3 copy-start.8
  155.9 1.3 copy-start.7
  156.2 1.3 copy-start.6
  156.6 1.3 copy-start.4
  158.1 1.2 copy-start.10
Sparse Core Ops, SparseCore 0:
  71.7 79.3 all-reduce.18
  154.6 107.7 all-reduce.16
